TPU v7x, 32 devices: a whole 2x2x4 slice. The times are simulated.
32 devices in a mesh: groups: 2 (over x), facet: 16 (over z, y, core).
Axes of the slice: x: 2, y: 2, z: 4, core: 2. Of those that a mesh axis runs over, the one named last changes fastest.
Arguments:
- facets: bfloat16 [32, 2, 512, 512], P(('groups', 'facet')), parts along dimension 0, may hold values from -6 to 6
- facet_offsets: int32 [32, 2], P(('groups', 'facet')), parts along dimension 0, may hold values from 0 to 511
- subgrid_offsets: int32 [32, 2], P('groups'), parts along dimension 0, may hold values from 0 to 511
- w_terms: float32 [32], P(('groups', 'facet')), parts along dimension 0, may hold values from 2 to 16
- tile_count: int32 [32], P(('groups', 'facet')), parts along dimension 0, may hold values from 1 to 16, as said below
- tile_offsets: int32 [512, 2], P(('groups', 'facet')), parts along dimension 0, may hold values from 0 to 256
- observed: bfloat16 [512, 2, 128, 128], P(('groups', 'facet')), parts along dimension 0, may hold values from -6 to 6
Outputs:
- residual: bfloat16 [512, 2, 128, 128], P(('groups', 'facet')), parts along dimension 0
- facet_update: bfloat16 [32, 2, 512, 512], P(('groups', 'facet')), parts along dimension 0
There are 2 independent parts, one for each index of `groups`. A program takes and returns all parts, laid end to end along the dimension named above; each array names one. Nothing has to cross between parts.
Inputs may be any that keep to these rules, and one draw needn't show every extreme that they name: `tile_count`: live tile slots of each subgrid; some subgrid has all 16 slots live in every draw.
All inputs are finite; a program needn't handle non-finite values.
Results may differ from a plain program's by a relative error of at most 0.017.
Values may be sent and summed in bfloat16 or wider, within the bound.
A program may use at most 64 MiB of HBM per device.

v0:
```python
import functools
import math

import jax
import jax.numpy as jnp
import ml_dtypes
import numpy as np
from jax import lax
from jax.experimental import pallas as pl
from jax.experimental.pallas import tpu as pltpu
from jax.sharding import PartitionSpec as P

F = 512
M = 128
SG = 512
TV = 128
SPAN = 384
WIDE = F + M
GROUP = 2

BF16 = jnp.bfloat16
F32 = jnp.float32
TWO_PI = 2.0 * math.pi
MESH = pl.DeviceIdType.MESH
VMEM = pltpu.VMEM
LIMIT = 48 * 1024 * 1024


def basis_table():
    index = np.arange(F)
    angle = -TWO_PI * (index[:, None] * index[None, :] % F) / F
    scale = 1.0 / math.sqrt(F)
    return np.stack([np.cos(angle) * scale, np.sin(angle) * scale]).astype(ml_dtypes.bfloat16)


def padding_table(facet_count):
    angle = TWO_PI * (np.arange(SG)[:, None] * np.arange(M)[None, :] % SG) / SG
    scale = (M * math.sqrt(facet_count)) ** (-0.5)
    return np.stack([np.cos(angle) * scale, np.sin(angle) * scale]).astype(ml_dtypes.bfloat16)


def taper_square():
    taper = 0.6 + 0.4 * np.sin(math.pi * (np.arange(M) + 0.5) / M)
    return (taper[:, None] * taper[None, :]).astype(np.float32)


def kernel_table():
    distance = np.arange(2 * TV)[None, :] - 2.0 * np.arange(TV)[:, None] - 1.0
    value = 0.75 * np.exp(-(distance / 1.5) * (distance / 1.5))
    return np.where(np.abs(distance) <= 4.0, value, 0.0).astype(ml_dtypes.bfloat16).astype(np.float32)


def dot(left, right):
    return jnp.dot(left, right, preferred_element_type=F32)


def dot_t(left, right):
    return lax.dot_general(left, right, (((1,), (1,)), ((), ())), preferred_element_type=F32)


def cos_sin_turns(turns):
    quarter = jnp.floor(turns * 4.0 + 0.5)
    y = (turns - quarter * 0.25) * TWO_PI
    y2 = y * y
    sine = y * (1.0 + y2 * (-1.0 / 6 + y2 * (1.0 / 120 + y2 * (-1.0 / 5040 + y2 * (1.0 / 362880)))))
    cosine = 1.0 + y2 * (
        -0.5 + y2 * (1.0 / 24 + y2 * (-1.0 / 720 + y2 * (1.0 / 40320 - y2 * (1.0 / 3628800))))
    )
    which = quarter.astype(jnp.int32) & 3
    odd = (which & 1) == 1
    first = jnp.where(odd, sine, cosine)
    second = jnp.where(odd, cosine, sine)
    cos_value = jnp.where((which == 1) | (which == 2), -first, first)
    sin_value = jnp.where(which >= 2, -second, second)
    return cos_value, sin_value


def tapered_phase(offset_ref, taper_ref):
    rows = lax.broadcasted_iota(jnp.int32, (M, M), 0)
    columns = lax.broadcasted_iota(jnp.int32, (M, M), 1)
    total = (rows * offset_ref[0, 0] + columns * offset_ref[0, 1]) & (F - 1)
    cos_value, sin_value = cos_sin_turns(total.astype(F32) * (1.0 / F))
    taper = taper_ref[...]
    return cos_value * taper, sin_value * taper


def forward_kernel(
    n, foff_h, soff_h, facet_h, basis_h, taper_h, out,
    half, spec, phase, foff, soff, facet, basis, taper, sems
):
    pairs = ((facet_h, facet), (basis_h, basis), (taper_h, taper), (foff_h, foff), (soff_h, soff))
    copies = [pltpu.make_async_copy(src, dst, sems.at[i]) for i, (src, dst) in enumerate(pairs)]
    for copy in copies:
        copy.start()
    for copy in copies:
        copy.wait()
    phase[0], phase[1] = tapered_phase(foff, taper)
    lanes = lax.broadcasted_iota(jnp.int32, (M, M), 1)

    @pl.loop(0, 2)
    def _(c):
        cols = pl.ds(pl.multiple_of(c * 256, 256), 256)
        br, bi = basis[0, :, cols], basis[1, :, cols]
        half[0, :, cols] = (dot(facet[0], br) - dot(facet[1], bi)).astype(BF16)
        half[1, :, cols] = (dot(facet[0], bi) + dot(facet[1], br)).astype(BF16)

    @pl.loop(0, 2)
    def _(c):
        cols = pl.ds(pl.multiple_of(c * 256, 256), 256)
        hr, hi = half[0, :, cols], half[1, :, cols]
        real = dot(basis[0], hr) - dot(basis[1], hi)
        imag = dot(basis[0], hi) + dot(basis[1], hr)
        for side in range(2):
            part = slice(side * M, side * M + M)
            spec[0, c * 2 + side, 0:F] = real[:, part]
            spec[1, c * 2 + side, 0:F] = imag[:, part]

    spec[:, 0 : F // M, F:WIDE] = spec[:, 0 : F // M, 0:M]
    spec[:, F // M] = spec[:, 0]

    @pl.loop(0, n)
    def _(s):
        sx, sy = soff[0, s], soff[1, s]
        tile, offset = sy >> 7, sy & 127
        shift = (M - offset) & 127
        kept = lanes < M - offset
        rows = pl.ds(sx, M)

        def window(plane):
            low = pltpu.roll(spec[plane, tile, rows], shift, 1)
            high = pltpu.roll(spec[plane, tile + 1, rows], shift, 1)
            return jnp.where(kept, low, high)

        real, imag = window(0), window(1)
        pc, ps = phase[0], phase[1]
        out[s & 1, (s >> 1) & 1, s >> 2, 0] = (pc * real - ps * imag).astype(BF16)
        out[s & 1, (s >> 1) & 1, s >> 2, 1] = (pc * imag + ps * real).astype(BF16)


def place(n):
    me = lax.axis_index("facet")
    quads = n // 4
    far_first = [1 + (t + quads // 2 - 1) % (quads - 1) for t in range(quads - 1)]
    return quads, me // 4, lax.rem(me // 2, 2), lax.rem(me, 2), far_first


def index(quad, middle, core):
    return quad * 4 + middle * 2 + core


def greet(peers):
    barrier = pltpu.get_barrier_semaphore()
    for peer in peers:
        pl.semaphore_signal(barrier, inc=1, device_id={"facet": peer}, device_id_type=MESH)
    pl.semaphore_wait(barrier, len(peers))


def send(src, dst, send_sem, recv_sem, peer):
    return pltpu.make_async_remote_copy(
        src_ref=src, dst_ref=dst, send_sem=send_sem, recv_sem=recv_sem,
        device_id={"facet": peer}, device_id_type=MESH,
    )


def reduce_kernel(
    n, contrib, summed, near, pair, mid, quad_sum, far,
    near_s, near_r, mid_s, mid_r, far_s, far_r
):
    quads, quad, middle, core, far_first = place(n)
    other = 1 - middle
    sibling, beside = index(quad, middle, 1 - core), index(quad, other, core)
    away = [lax.rem(quad + k, quads) for k in far_first]
    order = away + [quad]
    greet([index(j, middle, core) for j in away] + [beside, sibling])

    def near_copy(half, j):
        return send(contrib.at[1 - core, half, j], near.at[half, j], near_s.at[half, j], near_r.at[half, j], sibling)

    def mid_copy(j):
        return send(pair.at[j], mid.at[j], mid_s.at[j], mid_r.at[j], beside)

    def far_copy(j, slot):
        return send(quad_sum.at[j], far.at[slot], far_s.at[j], far_r.at[slot], index(j, middle, core))

    def near_sum(half, j):
        return contrib[core, half, j].astype(F32) + near[half, j].astype(F32)

    for half in (other, middle):
        for j in order:
            near_copy(half, j).start()
    for j in order:
        near_copy(other, j).wait_recv()
        pair[j] = near_sum(other, j).astype(BF16)
        mid_copy(j).start()
    for j in away:
        near_copy(middle, j).wait_recv()
        mid_copy(j).wait_recv()
        quad_sum[j] = (near_sum(middle, j) + mid[j].astype(F32)).astype(BF16)
        far_copy(j, quad).start()
    near_copy(middle, quad).wait_recv()
    mid_copy(quad).wait_recv()
    total = near_sum(middle, quad) + mid[quad].astype(F32)
    for j in reversed(away):
        far_copy(j, j).wait_recv()
        total = total + far[j].astype(F32)
    summed[...] = total
    for j in order:
        near_copy(other, j).wait_send()
        near_copy(middle, j).wait_send()
        mid_copy(j).wait_send()
    for j in away:
        far_copy(j, quad).wait_send()


def gather_kernel(n, mine, out, near_s, near_r, mid_s, mid_r, far_s, far_r, local):
    quads, quad, middle, core, far_first = place(n)
    other = 1 - middle
    me = index(quad, middle, core)
    sibling, beside = index(quad, middle, 1 - core), index(quad, other, core)
    away = [lax.rem(quad + k, quads) for k in far_first]
    back = [lax.rem(quad + quads - k, quads) for k in far_first]
    greet([index(j, middle, core) for j in away] + [beside, sibling])

    def far_copy(j, slot):
        return send(
            mine, out.at[index(slot, middle, core)], far_s.at[j], far_r.at[slot], index(j, middle, core)
        )

    def mid_copy(j, half):
        piece = out.at[index(j, half, core)]
        return send(piece, piece, mid_s.at[j], mid_r.at[j], beside)

    def near_copy(half, j, side):
        piece = out.at[index(j, half, side)]
        return send(piece, piece, near_s.at[half, j], near_r.at[half, j], sibling)

    for j in away:
        far_copy(j, quad).start()
    mid_own = send(mine, out.at[me], mid_s.at[quad], mid_r.at[quad], beside)
    mid_own.start()
    near_own = send(mine, out.at[me], near_s.at[middle, quad], near_r.at[middle, quad], sibling)
    near_own.start()
    own = pltpu.make_async_copy(mine, out.at[me], local)
    own.start()
    for j in back:
        far_copy(j, j).wait_recv()
        mid_copy(j, middle).start()
        near_copy(middle, j, core).start()
    for j in [quad] + back:
        mid_copy(j, other).wait_recv()
        near_copy(other, j, core).start()
    for half in (middle, other):
        for j in [quad] + back:
            near_copy(half, j, 1 - core).wait_recv()
    for j in away:
        far_copy(j, quad).wait_send()
        mid_copy(j, middle).wait_send()
        near_copy(middle, j, core).wait_send()
        near_copy(other, j, core).wait_send()
    near_copy(other, quad, core).wait_send()
    mid_own.wait_send()
    near_own.wait_send()
    own.wait()


def subgrid_kernel(
    slots, w_ref, count_ref, toff, summed, pad, pad_t, ker, ker_t, observed,
    residual, coefficient, inner, screen, model, adjoint, reduced, wide_t
):
    adjoint[...] = jnp.zeros_like(adjoint)
    residual[...] = jnp.zeros_like(residual)
    wide_t[...] = ker_t[...]
    sr, si = summed[0].astype(BF16), summed[1].astype(BF16)
    inner[0] = (dot(pad[0], sr) - dot(pad[1], si)).astype(BF16)
    inner[1] = (dot(pad[0], si) + dot(pad[1], sr)).astype(BF16)
    w_value = w_ref[0]

    @pl.loop(0, 4)
    def _(c):
        rows = pl.ds(pl.multiple_of(c * 128, 128), 128)
        u = (lax.broadcasted_iota(jnp.int32, (128, SG), 0) + (c * 128 - 256)).astype(F32)
        v = (lax.broadcasted_iota(jnp.int32, (128, SG), 1) - 256).astype(F32)
        radius = (u * u + v * v) * (1.0 / (SG * SG))
        cos_value, sin_value = cos_sin_turns(w_value * (jnp.sqrt(1.0 + radius) - 1.0))
        screen[0, rows, :] = cos_value
        screen[1, rows, :] = sin_value
        ir, ii = inner[0, rows, :], inner[1, rows, :]
        image_real = dot(ir, pad_t[0]) - dot(ii, pad_t[1])
        image_imag = dot(ir, pad_t[1]) + dot(ii, pad_t[0])
        model[0, rows, :] = (cos_value * image_real - sin_value * image_imag).astype(BF16)
        model[1, rows, :] = (cos_value * image_imag + sin_value * image_real).astype(BF16)

    count = count_ref[0]

    lanes = lax.broadcasted_iota(jnp.int32, (TV, TV), 1)
    blank = jnp.zeros((TV, TV), F32)

    def shifted(amount):
        low = pltpu.roll(ker[:, :TV], amount & 127, 1)
        high = pltpu.roll(ker[:, TV : 2 * TV], amount & 127, 1)
        inside = lanes >= amount
        return jnp.concatenate(
            [
                jnp.where(inside, low, blank).astype(BF16),
                jnp.where(inside, high, low).astype(BF16),
                jnp.where(inside, blank, high).astype(BF16),
            ],
            axis=1,
        )

    @pl.loop(0, (count + GROUP - 1) // GROUP)
    def _(step):
        slot = [step * GROUP + g for g in range(GROUP)]
        spans, ku, kv, kut = [], [], [], []
        for t in slot:
            ou, ov = toff[0, t], toff[1, t]
            u0 = pl.multiple_of(jnp.minimum(ou & ~127, 128), 128)
            v0 = pl.multiple_of(jnp.minimum(ov & ~127, 128), 128)
            spans.append((pl.ds(u0, SPAN), pl.ds(v0, SPAN)))
            ku.append(shifted(ou - u0))
            kv.append(shifted(ov - v0))
            kut.append(wide_t[pl.ds(128 - (ou - u0), SPAN), :].astype(BF16))
        left = [
            jnp.concatenate(
                [dot(ku[g], model[p, spans[g][0], spans[g][1]]).astype(BF16) for p in range(2)], axis=0
            )
            for g in range(GROUP)
        ]
        predicted = [dot_t(left[g], kv[g]) for g in range(GROUP)]
        rest = []
        for g, t in enumerate(slot):
            seen = observed[t].reshape(2 * TV, TV).astype(F32)
            value = (seen - predicted[g]).astype(BF16)
            rest.append(jnp.where(t < count, value, jnp.zeros_like(value)))
            residual[t] = rest[g].reshape(2, TV, TV)
        back = [dot(rest[g], kv[g]).astype(BF16) for g in range(GROUP)]
        spread = [[dot(kut[g], back[g][p * TV : p * TV + TV]) for p in range(2)] for g in range(GROUP)]
        for g in range(GROUP):
            for p in range(2):
                adjoint[p, spans[g][0], spans[g][1]] += spread[g][p]

    @pl.loop(0, 2)
    def _(c):
        cols = pl.ds(pl.multiple_of(c * 256, 256), 256)
        ar, ai = adjoint[0, :, cols], adjoint[1, :, cols]
        sc, ss = screen[0, :, cols], screen[1, :, cols]
        xr = (sc * ar + ss * ai).astype(BF16)
        xi = (sc * ai - ss * ar).astype(BF16)
        reduced[0, :, cols] = (dot(pad_t[0], xr) + dot(pad_t[1], xi)).astype(BF16)
        reduced[1, :, cols] = (dot(pad_t[0], xi) - dot(pad_t[1], xr)).astype(BF16)

    rr, ri = reduced[0], reduced[1]
    coefficient[0] = (dot(rr, pad[0]) + dot(ri, pad[1])).astype(BF16)
    coefficient[1] = (dot(ri, pad[0]) - dot(rr, pad[1])).astype(BF16)


def backward_kernel(n, foff, soff, piece, basis, taper, out, acc, spec, half, phase):
    phase[0], phase[1] = tapered_phase(foff, taper)
    lanes = lax.broadcasted_iota(jnp.int32, (M, M), 1)
    acc[...] = jnp.zeros_like(acc)

    @pl.loop(0, n)
    def _(s):
        sx, sy = soff[0, s], soff[1, s]
        tile, shift = sy >> 7, sy & 127
        rows = pl.ds(sx, M)
        kept = lanes >= shift
        pc, ps = phase[0], phase[1]
        real, imag = piece[s, 0].astype(F32), piece[s, 1].astype(F32)
        blank = jnp.zeros((M, M), F32)
        values = (pc * real + ps * imag, pc * imag - ps * real)
        for plane in range(2):
            turned = pltpu.roll(values[plane], shift, 1)
            acc[plane, tile, rows] += jnp.where(kept, turned, blank)
            acc[plane, tile + 1, rows] += jnp.where(kept, blank, turned)

    acc[:, 0] += acc[:, F // M]
    acc[:, 0 : F // M, 0:M] += acc[:, 0 : F // M, F:WIDE]
    for k in range(F // M):
        spec[:, :, k * M : k * M + M] = acc[:, k, 0:F].astype(BF16)

    @pl.loop(0, 2)
    def _(c):
        cols = pl.ds(pl.multiple_of(c * 256, 256), 256)
        xr, xi = spec[0, :, cols], spec[1, :, cols]
        half[0, :, cols] = (dot(basis[0], xr) + dot(basis[1], xi)).astype(BF16)
        half[1, :, cols] = (dot(basis[0], xi) - dot(basis[1], xr)).astype(BF16)

    @pl.loop(0, 2)
    def _(c):
        cols = pl.ds(pl.multiple_of(c * 256, 256), 256)
        br, bi = basis[0, :, cols], basis[1, :, cols]
        out[0, :, cols] = (dot(half[0], br) + dot(half[1], bi)).astype(BF16)
        out[1, :, cols] = (dot(half[1], br) - dot(half[0], bi)).astype(BF16)


SMEM_SPEC = pl.BlockSpec(memory_space=pltpu.SMEM)
VMEM_SPEC = pl.BlockSpec(memory_space=pltpu.VMEM)
HBM_SPEC = pl.BlockSpec(memory_space=pltpu.HBM)
DMA = pltpu.SemaphoreType.DMA


def per_device(facets, facet_offsets, subgrid_offsets, w_terms, tile_count, tile_offsets, observed):
    n = lax.axis_size("facet")
    quads = n // 4
    soff_t = subgrid_offsets.T
    slots = observed.shape[0]
    basis = jnp.asarray(basis_table())
    pad_np = padding_table(n)
    pad = jnp.asarray(pad_np)
    pad_t = jnp.asarray(np.ascontiguousarray(pad_np.transpose(0, 2, 1)))
    taper = jnp.asarray(taper_square())
    table = kernel_table()
    ker_t_np = np.zeros((4 * TV, TV), np.float32)
    ker_t_np[TV : 3 * TV] = table.T
    plain = pltpu.CompilerParams(vmem_limit_bytes=LIMIT)

    contrib = pl.pallas_call(
        functools.partial(forward_kernel, n),
        out_shape=jax.ShapeDtypeStruct((2, 2, quads, 2, M, M), BF16),
        in_specs=[HBM_SPEC] * 5,
        out_specs=VMEM_SPEC,
        scratch_shapes=[
            VMEM((2, F, F), BF16), VMEM((2, WIDE // M, WIDE, M), F32), VMEM((2, M, M), F32),
            pltpu.SMEM((1, 2), jnp.int32), pltpu.SMEM((2, n), jnp.int32),
            VMEM((2, F, F), BF16), VMEM((2, F, F), BF16), VMEM((M, M), F32), DMA((5,)),
        ],
        compiler_params=plain,
        name="forward",
    )(*[pltpu.with_memory_space_constraint(x, pltpu.HBM) for x in (facet_offsets, soff_t, facets[0], basis, taper)])

    summed = pl.pallas_call(
        functools.partial(reduce_kernel, n),
        out_shape=jax.ShapeDtypeStruct((2, M, M), F32),
        in_specs=[VMEM_SPEC],
        out_specs=VMEM_SPEC,
        scratch_shapes=[VMEM((2, quads, 2, M, M), BF16)]
        + [VMEM((quads, 2, M, M), BF16)] * 4
        + [DMA((2, quads))] * 2
        + [DMA((quads,))] * 4,
        compiler_params=pltpu.CompilerParams(
            vmem_limit_bytes=LIMIT, collective_id=0, has_side_effects=True
        ),
        name="reduce",
    )(contrib)

    residual, coefficient = pl.pallas_call(
        functools.partial(subgrid_kernel, slots),
        out_shape=(
            jax.ShapeDtypeStruct((slots, 2, TV, TV), BF16),
            jax.ShapeDtypeStruct((2, M, M), BF16),
        ),
        in_specs=[SMEM_SPEC] * 3 + [VMEM_SPEC] * 6,
        out_specs=(VMEM_SPEC, VMEM_SPEC),
        scratch_shapes=[
            VMEM((2, SG, M), BF16), VMEM((2, SG, SG), F32), VMEM((2, SG, SG), BF16),
            VMEM((2, SG, SG), F32), VMEM((2, M, SG), BF16), VMEM((4 * TV, TV), F32),
        ],
        compiler_params=plain,
        name="subgrid",
    )(
        w_terms, tile_count, tile_offsets.T, summed, pad, pad_t,
        jnp.asarray(table), jnp.asarray(ker_t_np), observed,
    )

    piece = pl.pallas_call(
        functools.partial(gather_kernel, n),
        out_shape=jax.ShapeDtypeStruct((n, 2, M, M), BF16),
        in_specs=[VMEM_SPEC],
        out_specs=VMEM_SPEC,
        scratch_shapes=[DMA((2, quads))] * 2 + [DMA((quads,))] * 4 + [DMA],
        compiler_params=pltpu.CompilerParams(
            vmem_limit_bytes=LIMIT, collective_id=1, has_side_effects=True
        ),
        name="gather",
    )(coefficient)

    update = pl.pallas_call(
        functools.partial(backward_kernel, n),
        out_shape=jax.ShapeDtypeStruct((2, F, F), BF16),
        in_specs=[SMEM_SPEC, SMEM_SPEC, VMEM_SPEC, VMEM_SPEC, VMEM_SPEC],
        out_specs=VMEM_SPEC,
        scratch_shapes=[
            VMEM((2, WIDE // M, WIDE, M), F32), VMEM((2, F, F), BF16), VMEM((2, F, F), BF16),
            VMEM((2, M, M), F32),
        ],
        compiler_params=plain,
        name="backward",
    )(facet_offsets, soff_t, piece, basis, taper)
    return (residual, update[None])


def solution(mesh):
    placed = (
        P(("groups", "facet"), None, None, None),
        P(("groups", "facet"), None),
        P("groups", None),
        P(("groups", "facet")),
        P(("groups", "facet")),
        P(("groups", "facet"), None),
        P(("groups", "facet"), None, None, None),
    )
    return jax.shard_map(
        per_device,
        mesh=mesh,
        in_specs=placed,
        out_specs=(
            P(("groups", "facet"), None, None, None),
            P(("groups", "facet"), None, None, None),
        ),
        check_vma=False,
    )
```

profile of v0, /device:TPU:0, one launch (start us, length us, event | category | flops | bytes accessed | tf_op | source)
XLA Modules:
  0.0 58.8 jit_solution(4825161050562241108)
XLA Ops:
  1.9 0.0 copy-start.2
  1.9 0.0 copy-start.3
  1.9 0.0 copy-start.4
  2.0 0.0 copy-start.9
  2.0 7.0 %forward.1.contrib = bf16[2,2,4,2,128,128]{5,4,3,2,1,0:T(8,128)(2,1)S(1)} custom-call(s32[1,2]{1,0:T(1,128)} %foff.1, s32[2,16]{1,0:T(2,128)} %bitcast.4, bf16[2,512,512]{2,1,0:T(8,128)(2,1)} %bitcast.7, bf16[2,512,512]{2,1,0:T(8,128)(2,1)} %constant.12.clone.basis_h.basis, f32[128,128]{1,0:T(8,128)} %constant.15.clone.taper_h.taper), custom_call_target="tpu_custom_call" | custom-call | tf_op jit(solution)/shard_map/forward/pallas_call | solution.py:418
  9.0 0.0 copy-start.1
  9.0 0.0 copy-start.6
  9.0 17.3 %reduce.1.summed = f32[2,128,128]{2,1,0:T(8,128)S(1)} custom-call(bf16[2,2,4,2,128,128]{5,4,3,2,1,0:T(8,128)(2,1)S(1)} %forward.1.contrib), custom_call_target="tpu_custom_call" | custom-call | tf_op jit(solution)/shard_map/reduce/pallas_call | solution.py:432
  26.2 0.0 copy-done.2
  26.3 0.0 copy-done.3
  26.3 0.0 copy-done.4
  26.3 0.0 copy-done.9
  26.3 0.0 copy-done.1
  26.3 0.0 copy-done.6
  26.3 7.4 %subgrid.1 = (bf16[16,2,128,128]{3,2,1,0:T(8,128)(2,1)}, bf16[2,128,128]{2,1,0:T(8,128)(2,1)S(1)}) custom-call(f32[1]{0:T(128)S(6)} %copy.15.w_ref, s32[1]{0:T(128)S(6)} %copy.16.count_ref, s32[2,16]{1,0:T(2,128)S(1)} %bitcast.6, f32[2,128,128]{2,1,0:T(8,128)S(1)} %reduce.1.summed, bf16[2,512,128]{2,1,0:T(8,128)(2,1)S(1)} %copy-done.4, ...), custom_call_target="tpu_custom_call" | custom-call | tf_op jit(solution)/shard_map/subgrid/pallas_call | solution.py:447
  33.7 0.0 copy-start
  33.7 0.0 copy-start.5
  33.7 0.0 copy-start.7
  33.7 0.0 copy-start.8
  33.8 18.3 %gather.1.piece = bf16[16,2,128,128]{3,2,1,0:T(8,128)(2,1)S(1)} custom-call(bf16[2,128,128]{2,1,0:T(8,128)(2,1)S(1)} %get-tuple-element.5.mine), custom_call_target="tpu_custom_call" | custom-call | tf_op jit(solution)/shard_map/gather/pallas_call | solution.py:466
  52.0 0.0 copy-done
  52.0 0.0 copy-done.5
  52.0 0.0 copy-done.7
  52.1 0.0 copy-done.8
  52.1 6.7 %backward.1 = bf16[2,512,512]{2,1,0:T(8,128)(2,1)} custom-call(s32[1,2]{1,0:T(1,128)S(1)} %copy-done.8, s32[2,16]{1,0:T(2,128)S(1)} %bitcast.5, bf16[16,2,128,128]{3,2,1,0:T(8,128)(2,1)S(1)} %gather.1.piece, bf16[2,512,512]{2,1,0:T(8,128)(2,1)S(1)} %copy-done, f32[128,128]{1,0:T(8,128)S(1)} %copy-done.5), custom_call_target="tpu_custom_call" | custom-call | tf_op jit(solution)/shard_map/backward/pallas_call | solution.py:478
Async XLA Ops:
  1.9 24.3 %copy-start.2 = (f32[512,128]{1,0:T(8,128)S(1)}, f32[512,128]{1,0:T(8,128)}, u32[]{:S(2)}) copy-start(f32[512,128]{1,0:T(8,128)} %constant.17.clone.ker_t) | copy-start | bytes 786436
  1.9 24.3 %copy-start.3 = (bf16[2,128,512]{2,1,0:T(8,128)(2,1)S(1)}, bf16[2,128,512]{2,1,0:T(8,128)(2,1)}, u32[]{:S(2)}) copy-start(bf16[2,128,512]{2,1,0:T(8,128)(2,1)} %constant.14.clone.pad_t) | copy-start | bytes 786436
  1.9 24.3 %copy-start.4 = (bf16[2,512,128]{2,1,0:T(8,128)(2,1)S(1)}, bf16[2,512,128]{2,1,0:T(8,128)(2,1)}, u32[]{:S(2)}) copy-start(bf16[2,512,128]{2,1,0:T(8,128)(2,1)} %constant.13.clone.pad) | copy-start | bytes 786436
  2.0 24.3 %copy-start.9 = (s32[16,2]{0,1:T(2,128)S(1)}, s32[16,2]{0,1:T(2,128)}, u32[]{:S(2)}) copy-start(s32[16,2]{0,1:T(2,128)} %param.18) | copy-start | bytes 388
  9.0 17.3 %copy-start.1 = (bf16[16,2,128,128]{3,2,1,0:T(8,128)(2,1)S(1)}, bf16[16,2,128,128]{3,2,1,0:T(8,128)(2,1)}, u32[]{:S(2)}) copy-start(bf16[16,2,128,128]{3,2,1,0:T(8,128)(2,1)} %observed.1) | copy-start | bytes 3145732
  9.0 17.3 %copy-start.6 = (f32[128,256]{1,0:T(8,128)S(1)}, f32[128,256]{1,0:T(8,128)}, u32[]{:S(2)}) copy-start(f32[128,256]{1,0:T(8,128)} %constant.16.clone.ker) | copy-start | bytes 393220
  33.7 18.3 %copy-start = (bf16[2,512,512]{2,1,0:T(8,128)(2,1)S(1)}, bf16[2,512,512]{2,1,0:T(8,128)(2,1)}, u32[]{:S(2)}) copy-start(bf16[2,512,512]{2,1,0:T(8,128)(2,1)} %constant.12.clone.basis_h.basis) | copy-start | bytes 3145732
  33.7 18.3 %copy-start.5 = (f32[128,128]{1,0:T(8,128)S(1)}, f32[128,128]{1,0:T(8,128)}, u32[]{:S(2)}) copy-start(f32[128,128]{1,0:T(8,128)} %constant.15.clone.taper_h.taper) | copy-start | bytes 196612
  33.7 18.3 %copy-start.7 = (s32[16,2]{0,1:T(2,128)S(1)}, s32[16,2]{0,1:T(2,128)}, u32[]{:S(2)}) copy-start(s32[16,2]{0,1:T(2,128)} %param.15) | copy-start | bytes 388
  33.7 18.3 %copy-start.8 = (s32[1,2]{1,0:T(1,128)S(1)}, s32[1,2]{1,0:T(1,128)}, u32[]{:S(2)}) copy-start(s32[1,2]{1,0:T(1,128)} %foff.1) | copy-start | bytes 28
where the time goes:
time: 58.9 us; the launch traced here: 58.8 us
  Pallas kernels  56.6 us (96%)
  between operations  2.08 us (4%)
    pallas_call x1, Pallas kernels, per_device(): pl.pallas_call(functools.partial(gather_kernel, n), out_shape=jax.ShapeDt...  18.3 us
    pallas_call x1, Pallas kernels, per_device(): pl.pallas_call(functools.partial(reduce_kernel, n), out_shape=jax.ShapeDt...  17.3 us
    pallas_call x1, Pallas kernels, per_device(): pl.pallas_call(functools.partial(subgrid_kernel, slots), out_shape=(jax.S...  7.43 us
    pallas_call x1, Pallas kernels, per_device(): pl.pallas_call(functools.partial(forward_kernel, n), out_shape=jax.ShapeD...  6.98 us
    pallas_call x1, Pallas kernels, per_device(): pl.pallas_call(functools.partial(backward_kernel, n), out_shape=jax.Shape...  6.71 us

commit v1 on v0

--- a/solution.py
+++ b/solution.py
@@ -16,7 +16,7 @@
 TV = 128
 SPAN = 384
 WIDE = F + M
-GROUP = 2
+GROUP = 4
 
 BF16 = jnp.bfloat16
 F32 = jnp.float32
@@ -162,8 +162,20 @@
     )
 
 
+def fill_screen(w_value, screen):
+    @pl.loop(0, 4)
+    def _(c):
+        rows = pl.ds(pl.multiple_of(c * 128, 128), 128)
+        u = (lax.broadcasted_iota(jnp.int32, (128, SG), 0) + (c * 128 - 256)).astype(F32)
+        v = (lax.broadcasted_iota(jnp.int32, (128, SG), 1) - 256).astype(F32)
+        radius = (u * u + v * v) * (1.0 / (SG * SG))
+        cos_value, sin_value = cos_sin_turns(w_value * (jnp.sqrt(1.0 + radius) - 1.0))
+        screen[0, rows, :] = cos_value
+        screen[1, rows, :] = sin_value
+
+
 def reduce_kernel(
-    n, contrib, summed, near, pair, mid, quad_sum, far,
+    n, w_ref, contrib, summed, screen, near, pair, mid, quad_sum, far,
     near_s, near_r, mid_s, mid_r, far_s, far_r
 ):
     quads, quad, middle, core, far_first = place(n)
@@ -197,6 +209,7 @@
         mid_copy(j).wait_recv()
         quad_sum[j] = (near_sum(middle, j) + mid[j].astype(F32)).astype(BF16)
         far_copy(j, quad).start()
+    fill_screen(w_ref[0], screen)
     near_copy(middle, quad).wait_recv()
     mid_copy(quad).wait_recv()
     total = near_sum(middle, quad) + mid[quad].astype(F32)
@@ -264,8 +277,8 @@
 
 
 def subgrid_kernel(
-    slots, w_ref, count_ref, toff, summed, pad, pad_t, ker, ker_t, observed,
-    residual, coefficient, inner, screen, model, adjoint, reduced, wide_t
+    slots, count_ref, toff, summed, screen, pad, pad_t, ker, ker_t, observed,
+    residual, coefficient, inner, model, adjoint, reduced, wide_t
 ):
     adjoint[...] = jnp.zeros_like(adjoint)
     residual[...] = jnp.zeros_like(residual)
@@ -273,17 +286,11 @@
     sr, si = summed[0].astype(BF16), summed[1].astype(BF16)
     inner[0] = (dot(pad[0], sr) - dot(pad[1], si)).astype(BF16)
     inner[1] = (dot(pad[0], si) + dot(pad[1], sr)).astype(BF16)
-    w_value = w_ref[0]
 
     @pl.loop(0, 4)
     def _(c):
         rows = pl.ds(pl.multiple_of(c * 128, 128), 128)
-        u = (lax.broadcasted_iota(jnp.int32, (128, SG), 0) + (c * 128 - 256)).astype(F32)
-        v = (lax.broadcasted_iota(jnp.int32, (128, SG), 1) - 256).astype(F32)
-        radius = (u * u + v * v) * (1.0 / (SG * SG))
-        cos_value, sin_value = cos_sin_turns(w_value * (jnp.sqrt(1.0 + radius) - 1.0))
-        screen[0, rows, :] = cos_value
-        screen[1, rows, :] = sin_value
+        cos_value, sin_value = screen[0, rows, :], screen[1, rows, :]
         ir, ii = inner[0, rows, :], inner[1, rows, :]
         image_real = dot(ir, pad_t[0]) - dot(ii, pad_t[1])
         image_imag = dot(ir, pad_t[1]) + dot(ii, pad_t[0])
@@ -429,11 +436,13 @@
         name="forward",
     )(*[pltpu.with_memory_space_constraint(x, pltpu.HBM) for x in (facet_offsets, soff_t, facets[0], basis, taper)])
 
-    summed = pl.pallas_call(
+    summed, screen = pl.pallas_call(
         functools.partial(reduce_kernel, n),
-        out_shape=jax.ShapeDtypeStruct((2, M, M), F32),
-        in_specs=[VMEM_SPEC],
-        out_specs=VMEM_SPEC,
+        out_shape=(
+            jax.ShapeDtypeStruct((2, M, M), F32), jax.ShapeDtypeStruct((2, SG, SG), F32),
+        ),
+        in_specs=[SMEM_SPEC, VMEM_SPEC],
+        out_specs=(VMEM_SPEC, VMEM_SPEC),
         scratch_shapes=[VMEM((2, quads, 2, M, M), BF16)]
         + [VMEM((quads, 2, M, M), BF16)] * 4
         + [DMA((2, quads))] * 2
@@ -442,7 +451,7 @@
             vmem_limit_bytes=LIMIT, collective_id=0, has_side_effects=True
         ),
         name="reduce",
-    )(contrib)
+    )(w_terms, contrib)
 
     residual, coefficient = pl.pallas_call(
         functools.partial(subgrid_kernel, slots),
@@ -450,16 +459,16 @@
             jax.ShapeDtypeStruct((slots, 2, TV, TV), BF16),
             jax.ShapeDtypeStruct((2, M, M), BF16),
         ),
-        in_specs=[SMEM_SPEC] * 3 + [VMEM_SPEC] * 6,
+        in_specs=[SMEM_SPEC] * 2 + [VMEM_SPEC] * 7,
         out_specs=(VMEM_SPEC, VMEM_SPEC),
         scratch_shapes=[
-            VMEM((2, SG, M), BF16), VMEM((2, SG, SG), F32), VMEM((2, SG, SG), BF16),
+            VMEM((2, SG, M), BF16), VMEM((2, SG, SG), BF16),
             VMEM((2, SG, SG), F32), VMEM((2, M, SG), BF16), VMEM((4 * TV, TV), F32),
         ],
         compiler_params=plain,
         name="subgrid",
     )(
-        w_terms, tile_count, tile_offsets.T, summed, pad, pad_t,
+        tile_count, tile_offsets.T, summed, screen, pad, pad_t,
         jnp.asarray(table), jnp.asarray(ker_t_np), observed,
     )
 

time: 58.9 us -> 56.4 us (0.958)
  Pallas kernels: 56.6 us -> 53.9 us
    pallas_call x1, Pallas kernels: 18.3 us -> 13.2 us  [per_device(): pl.pallas_call(functools.partial(gather_kernel, n), out_shape=jax.ShapeDt...]
    pallas_call x1, Pallas kernels: 7.43 us -> 9.72 us  [per_device(): pl.pallas_call(functools.partial(subgrid_kernel, slots), out_shape=(jax.S...]
where the time goes in v1:
time: 56.4 us; the launch traced here: 56.1 us
  Pallas kernels  53.9 us (96%)
  between operations  2.1 us (4%)
    pallas_call x1, Pallas kernels, per_device(): pl.pallas_call(functools.partial(reduce_kernel, n), out_shape=(jax.ShapeD...  17.3 us
    pallas_call x1, Pallas kernels, per_device(): pl.pallas_call(functools.partial(gather_kernel, n), out_shape=jax.ShapeDt...  13.2 us
    pallas_call x1, Pallas kernels, per_device(): pl.pallas_call(functools.partial(subgrid_kernel, slots), out_shape=(jax.S...  9.72 us
    pallas_call x1, Pallas kernels, per_device(): pl.pallas_call(functools.partial(forward_kernel, n), out_shape=jax.ShapeD...  7.04 us
    pallas_call x1, Pallas kernels, per_device(): pl.pallas_call(functools.partial(backward_kernel, n), out_shape=jax.Shape...  6.71 us

profile of v1, /device:TPU:0, one launch (start us, length us, event | category | flops | bytes accessed | tf_op | source)
XLA Modules:
  0.0 56.1 jit_solution(14491793921343542460)
XLA Ops:
  1.9 0.0 copy-start.1
  1.9 0.0 copy-start.2
  1.9 0.0 copy-start.3
  2.0 0.0 copy-start.4
  2.0 0.0 copy-start.6
  2.0 0.0 copy-start.9
  2.0 7.0 %forward.1.contrib = bf16[2,2,4,2,128,128]{5,4,3,2,1,0:T(8,128)(2,1)S(1)} custom-call(s32[1,2]{1,0:T(1,128)} %foff.1, s32[2,16]{1,0:T(2,128)} %bitcast.4, bf16[2,512,512]{2,1,0:T(8,128)(2,1)} %bitcast.7, bf16[2,512,512]{2,1,0:T(8,128)(2,1)} %constant.12.clone.basis_h.basis, f32[128,128]{1,0:T(8,128)} %constant.15.clone.taper_h.taper), custom_call_target="tpu_custom_call" | custom-call | tf_op jit(solution)/shard_map/forward/pallas_call | solution.py:425
  9.0 17.3 %reduce.1 = (f32[2,128,128]{2,1,0:T(8,128)S(1)}, f32[2,512,512]{2,1,0:T(8,128)S(1)}) custom-call(f32[1]{0:T(128)S(6)} %copy.15.w_ref, bf16[2,2,4,2,128,128]{5,4,3,2,1,0:T(8,128)(2,1)S(1)} %forward.1.contrib), custom_call_target="tpu_custom_call" | custom-call | tf_op jit(solution)/shard_map/reduce/pallas_call | solution.py:439
  26.3 0.0 copy-done.1
  26.3 0.0 copy-done.2
  26.3 0.0 copy-done.3
  26.3 0.0 copy-done.4
  26.4 0.0 copy-done.6
  26.4 0.0 copy-done.9
  26.4 0.0 copy-start
  26.4 0.0 copy-start.5
  26.4 0.0 copy-start.7
  26.4 0.0 copy-start.8
  26.4 9.7 %subgrid.1 = (bf16[16,2,128,128]{3,2,1,0:T(8,128)(2,1)}, bf16[2,128,128]{2,1,0:T(8,128)(2,1)S(1)}) custom-call(s32[1]{0:T(128)S(6)} %copy.16.count_ref, s32[2,16]{1,0:T(2,128)S(1)} %bitcast.6, f32[2,128,128]{2,1,0:T(8,128)S(1)} %get-tuple-element.6.summed, f32[2,512,512]{2,1,0:T(8,128)S(1)} %get-tuple-element.7.screen, bf16[2,512,128]{2,1,0:T(8,128)(2,1)S(1)} %copy-done.4, ...), custom_call_target="tpu_custom_call" | custom-call | tf_op jit(solution)/shard_map/subgrid/pallas_call | solution.py:456
  36.1 13.2 %gather.1.piece = bf16[16,2,128,128]{3,2,1,0:T(8,128)(2,1)S(1)} custom-call(bf16[2,128,128]{2,1,0:T(8,128)(2,1)S(1)} %get-tuple-element.9.mine), custom_call_target="tpu_custom_call" | custom-call | tf_op jit(solution)/shard_map/gather/pallas_call | solution.py:475
  49.3 0.0 copy-done
  49.3 0.0 copy-done.5
  49.3 0.0 copy-done.7
  49.3 0.0 copy-done.8
  49.4 6.7 %backward.1 = bf16[2,512,512]{2,1,0:T(8,128)(2,1)} custom-call(s32[1,2]{1,0:T(1,128)S(1)} %copy-done.8, s32[2,16]{1,0:T(2,128)S(1)} %bitcast.5, bf16[16,2,128,128]{3,2,1,0:T(8,128)(2,1)S(1)} %gather.1.piece, bf16[2,512,512]{2,1,0:T(8,128)(2,1)S(1)} %copy-done, f32[128,128]{1,0:T(8,128)S(1)} %copy-done.5), custom_call_target="tpu_custom_call" | custom-call | tf_op jit(solution)/shard_map/backward/pallas_call | solution.py:487
Async XLA Ops:
  1.9 24.4 %copy-start.1 = (bf16[16,2,128,128]{3,2,1,0:T(8,128)(2,1)S(1)}, bf16[16,2,128,128]{3,2,1,0:T(8,128)(2,1)}, u32[]{:S(2)}) copy-start(bf16[16,2,128,128]{3,2,1,0:T(8,128)(2,1)} %observed.1) | copy-start | bytes 3145732
  1.9 24.4 %copy-start.2 = (f32[512,128]{1,0:T(8,128)S(1)}, f32[512,128]{1,0:T(8,128)}, u32[]{:S(2)}) copy-start(f32[512,128]{1,0:T(8,128)} %constant.17.clone.ker_t) | copy-start | bytes 786436
  1.9 24.4 %copy-start.3 = (bf16[2,128,512]{2,1,0:T(8,128)(2,1)S(1)}, bf16[2,128,512]{2,1,0:T(8,128)(2,1)}, u32[]{:S(2)}) copy-start(bf16[2,128,512]{2,1,0:T(8,128)(2,1)} %constant.14.clone.pad_t) | copy-start | bytes 786436
  2.0 24.4 %copy-start.4 = (bf16[2,512,128]{2,1,0:T(8,128)(2,1)S(1)}, bf16[2,512,128]{2,1,0:T(8,128)(2,1)}, u32[]{:S(2)}) copy-start(bf16[2,512,128]{2,1,0:T(8,128)(2,1)} %constant.13.clone.pad) | copy-start | bytes 786436
  2.0 24.4 %copy-start.6 = (f32[128,256]{1,0:T(8,128)S(1)}, f32[128,256]{1,0:T(8,128)}, u32[]{:S(2)}) copy-start(f32[128,256]{1,0:T(8,128)} %constant.16.clone.ker) | copy-start | bytes 393220
  2.0 24.4 %copy-start.9 = (s32[16,2]{0,1:T(2,128)S(1)}, s32[16,2]{0,1:T(2,128)}, u32[]{:S(2)}) copy-start(s32[16,2]{0,1:T(2,128)} %param.18) | copy-start | bytes 388
  26.4 22.9 %copy-start = (bf16[2,512,512]{2,1,0:T(8,128)(2,1)S(1)}, bf16[2,512,512]{2,1,0:T(8,128)(2,1)}, u32[]{:S(2)}) copy-start(bf16[2,512,512]{2,1,0:T(8,128)(2,1)} %constant.12.clone.basis_h.basis) | copy-start | bytes 3145732
  26.4 22.9 %copy-start.5 = (f32[128,128]{1,0:T(8,128)S(1)}, f32[128,128]{1,0:T(8,128)}, u32[]{:S(2)}) copy-start(f32[128,128]{1,0:T(8,128)} %constant.15.clone.taper_h.taper) | copy-start | bytes 196612
  26.4 22.9 %copy-start.7 = (s32[16,2]{0,1:T(2,128)S(1)}, s32[16,2]{0,1:T(2,128)}, u32[]{:S(2)}) copy-start(s32[16,2]{0,1:T(2,128)} %param.15) | copy-start | bytes 388
  26.4 22.9 %copy-start.8 = (s32[1,2]{1,0:T(1,128)S(1)}, s32[1,2]{1,0:T(1,128)}, u32[]{:S(2)}) copy-start(s32[1,2]{1,0:T(1,128)} %foff.1) | copy-start | bytes 28

commit v2 on v1

--- a/solution.py
+++ b/solution.py
@@ -118,7 +118,7 @@
     spec[:, 0 : F // M, F:WIDE] = spec[:, 0 : F // M, 0:M]
     spec[:, F // M] = spec[:, 0]
 
-    @pl.loop(0, n)
+    @pl.loop(0, n, unroll=4)
     def _(s):
         sx, sy = soff[0, s], soff[1, s]
         tile, offset = sy >> 7, sy & 127
@@ -366,7 +366,7 @@
     lanes = lax.broadcasted_iota(jnp.int32, (M, M), 1)
     acc[...] = jnp.zeros_like(acc)
 
-    @pl.loop(0, n)
+    @pl.loop(0, n, unroll=4)
     def _(s):
         sx, sy = soff[0, s], soff[1, s]
         tile, shift = sy >> 7, sy & 127

time: 56.4 us -> 55.9 us (level)
    pallas_call x1, Pallas kernels: 13.2 us -> 18.3 us  [per_device(): pl.pallas_call(functools.partial(gather_kernel, n), out_shape=jax.ShapeDt...]
    pallas_call x1, Pallas kernels: 9.72 us -> 6.06 us  [per_device(): pl.pallas_call(functools.partial(subgrid_kernel, slots), out_shape=(jax.S...]
    pallas_call x1, Pallas kernels: 7.04 us -> 6.19 us  [per_device(): pl.pallas_call(functools.partial(forward_kernel, n), out_shape=jax.ShapeD...]
    pallas_call x1, Pallas kernels: 6.71 us -> 5.91 us  [per_device(): pl.pallas_call(functools.partial(backward_kernel, n), out_shape=jax.Shape...]
where the time goes in v2:
time: 55.9 us; the launch traced here: 55.8 us
  Pallas kernels  53.7 us (96%)
  between operations  2.1 us (4%)
    pallas_call x1, Pallas kernels, per_device(): pl.pallas_call(functools.partial(gather_kernel, n), out_shape=jax.ShapeDt...  18.3 us
    pallas_call x1, Pallas kernels, per_device(): pl.pallas_call(functools.partial(reduce_kernel, n), out_shape=(jax.ShapeD...  17.3 us
    pallas_call x1, Pallas kernels, per_device(): pl.pallas_call(functools.partial(forward_kernel, n), out_shape=jax.ShapeD...  6.19 us
    pallas_call x1, Pallas kernels, per_device(): pl.pallas_call(functools.partial(subgrid_kernel, slots), out_shape=(jax.S...  6.06 us
    pallas_call x1, Pallas kernels, per_device(): pl.pallas_call(functools.partial(backward_kernel, n), out_shape=jax.Shape...  5.91 us

profile of v2, /device:TPU:0, one launch (start us, length us, event | category | flops | bytes accessed | tf_op | source)
XLA Modules:
  0.0 55.8 jit_solution(10441350030569960243)
XLA Ops:
  1.9 0.0 copy-start.1
  1.9 0.0 copy-start.2
  1.9 0.0 copy-start.3
  2.0 0.0 copy-start.4
  2.0 0.0 copy-start.6
  2.0 0.0 copy-start.9
  2.0 6.2 %forward.1.contrib = bf16[2,2,4,2,128,128]{5,4,3,2,1,0:T(8,128)(2,1)S(1)} custom-call(s32[1,2]{1,0:T(1,128)} %foff.1, s32[2,16]{1,0:T(2,128)} %bitcast.4, bf16[2,512,512]{2,1,0:T(8,128)(2,1)} %bitcast.7, bf16[2,512,512]{2,1,0:T(8,128)(2,1)} %constant.12.clone.basis_h.basis, f32[128,128]{1,0:T(8,128)} %constant.15.clone.taper_h.taper), custom_call_target="tpu_custom_call" | custom-call | tf_op jit(solution)/shard_map/forward/pallas_call | solution.py:425
  8.2 17.3 %reduce.1 = (f32[2,128,128]{2,1,0:T(8,128)S(1)}, f32[2,512,512]{2,1,0:T(8,128)S(1)}) custom-call(f32[1]{0:T(128)S(6)} %copy.15.w_ref, bf16[2,2,4,2,128,128]{5,4,3,2,1,0:T(8,128)(2,1)S(1)} %forward.1.contrib), custom_call_target="tpu_custom_call" | custom-call | tf_op jit(solution)/shard_map/reduce/pallas_call | solution.py:439
  25.5 0.0 copy-done.1
  25.5 0.0 copy-done.2
  25.5 0.0 copy-done.3
  25.5 0.0 copy-done.4
  25.5 0.0 copy-done.6
  25.5 0.0 copy-done.9
  25.5 0.0 copy-start
  25.5 0.0 copy-start.5
  25.5 0.0 copy-start.7
  25.6 0.0 copy-start.8
  25.6 6.1 %subgrid.1 = (bf16[16,2,128,128]{3,2,1,0:T(8,128)(2,1)}, bf16[2,128,128]{2,1,0:T(8,128)(2,1)S(1)}) custom-call(s32[1]{0:T(128)S(6)} %copy.16.count_ref, s32[2,16]{1,0:T(2,128)S(1)} %bitcast.6, f32[2,128,128]{2,1,0:T(8,128)S(1)} %get-tuple-element.6.summed, f32[2,512,512]{2,1,0:T(8,128)S(1)} %get-tuple-element.7.screen, bf16[2,512,128]{2,1,0:T(8,128)(2,1)S(1)} %copy-done.4, ...), custom_call_target="tpu_custom_call" | custom-call | tf_op jit(solution)/shard_map/subgrid/pallas_call | solution.py:456
  31.6 18.3 %gather.1.piece = bf16[16,2,128,128]{3,2,1,0:T(8,128)(2,1)S(1)} custom-call(bf16[2,128,128]{2,1,0:T(8,128)(2,1)S(1)} %get-tuple-element.9.mine), custom_call_target="tpu_custom_call" | custom-call | tf_op jit(solution)/shard_map/gather/pallas_call | solution.py:475
  49.9 0.0 copy-done
  49.9 0.0 copy-done.5
  49.9 0.0 copy-done.7
  49.9 0.0 copy-done.8
  49.9 5.9 %backward.1 = bf16[2,512,512]{2,1,0:T(8,128)(2,1)} custom-call(s32[1,2]{1,0:T(1,128)S(1)} %copy-done.8, s32[2,16]{1,0:T(2,128)S(1)} %bitcast.5, bf16[16,2,128,128]{3,2,1,0:T(8,128)(2,1)S(1)} %gather.1.piece, bf16[2,512,512]{2,1,0:T(8,128)(2,1)S(1)} %copy-done, f32[128,128]{1,0:T(8,128)S(1)} %copy-done.5), custom_call_target="tpu_custom_call" | custom-call | tf_op jit(solution)/shard_map/backward/pallas_call | solution.py:487
Async XLA Ops:
  1.9 23.5 %copy-start.1 = (bf16[16,2,128,128]{3,2,1,0:T(8,128)(2,1)S(1)}, bf16[16,2,128,128]{3,2,1,0:T(8,128)(2,1)}, u32[]{:S(2)}) copy-start(bf16[16,2,128,128]{3,2,1,0:T(8,128)(2,1)} %observed.1) | copy-start | bytes 3145732
  1.9 23.5 %copy-start.2 = (f32[512,128]{1,0:T(8,128)S(1)}, f32[512,128]{1,0:T(8,128)}, u32[]{:S(2)}) copy-start(f32[512,128]{1,0:T(8,128)} %constant.17.clone.ker_t) | copy-start | bytes 786436
  1.9 23.5 %copy-start.3 = (bf16[2,128,512]{2,1,0:T(8,128)(2,1)S(1)}, bf16[2,128,512]{2,1,0:T(8,128)(2,1)}, u32[]{:S(2)}) copy-start(bf16[2,128,512]{2,1,0:T(8,128)(2,1)} %constant.14.clone.pad_t) | copy-start | bytes 786436
  2.0 23.5 %copy-start.4 = (bf16[2,512,128]{2,1,0:T(8,128)(2,1)S(1)}, bf16[2,512,128]{2,1,0:T(8,128)(2,1)}, u32[]{:S(2)}) copy-start(bf16[2,512,128]{2,1,0:T(8,128)(2,1)} %constant.13.clone.pad) | copy-start | bytes 786436
  2.0 23.5 %copy-start.6 = (f32[128,256]{1,0:T(8,128)S(1)}, f32[128,256]{1,0:T(8,128)}, u32[]{:S(2)}) copy-start(f32[128,256]{1,0:T(8,128)} %constant.16.clone.ker) | copy-start | bytes 393220
  2.0 23.5 %copy-start.9 = (s32[16,2]{0,1:T(2,128)S(1)}, s32[16,2]{0,1:T(2,128)}, u32[]{:S(2)}) copy-start(s32[16,2]{0,1:T(2,128)} %param.18) | copy-start | bytes 388
  25.5 24.4 %copy-start = (bf16[2,512,512]{2,1,0:T(8,128)(2,1)S(1)}, bf16[2,512,512]{2,1,0:T(8,128)(2,1)}, u32[]{:S(2)}) copy-start(bf16[2,512,512]{2,1,0:T(8,128)(2,1)} %constant.12.clone.basis_h.basis) | copy-start | bytes 3145732
  25.5 24.4 %copy-start.5 = (f32[128,128]{1,0:T(8,128)S(1)}, f32[128,128]{1,0:T(8,128)}, u32[]{:S(2)}) copy-start(f32[128,128]{1,0:T(8,128)} %constant.15.clone.taper_h.taper) | copy-start | bytes 196612
  25.5 24.4 %copy-start.7 = (s32[16,2]{0,1:T(2,128)S(1)}, s32[16,2]{0,1:T(2,128)}, u32[]{:S(2)}) copy-start(s32[16,2]{0,1:T(2,128)} %param.15) | copy-start | bytes 388
  25.6 24.4 %copy-start.8 = (s32[1,2]{1,0:T(1,128)S(1)}, s32[1,2]{1,0:T(1,128)}, u32[]{:S(2)}) copy-start(s32[1,2]{1,0:T(1,128)} %foff.1) | copy-start | bytes 28
